TPU v7x, 32 devices: a whole 2x2x4 slice. The times are simulated.
32 devices in a mesh: dp: 4 (over y, x), expert: 4 (over z), tensor: 2 (over core).
Axes of the slice: x: 2, y: 2, z: 4, core: 2. Of those that a mesh axis runs over, the one named last changes fastest.
Arguments:
- tokens: bfloat16 [4096, 2048], P(('dp', 'expert')), may hold values from -6 to 6
- segments: int32 [4, 1024], P('dp', 'expert'), may hold values from 0 to 7, never falling along the last dimension, each value on 1 to 512 neighbouring positions
- routes: int32 [4096, 4], P(('dp', 'expert')), may hold values from 0 to 7, all different within a row; in each aligned block of 256 rows (0 to 255, 256 to 511, ...) at most 192 rows name the same one
- norm1_gain: bfloat16 [2048], replicated, may hold values from 0.5 to 1.5
- q_weight: bfloat16 [2048, 2048], P(None, 'tensor'), may hold values from -0.125 to 0.125
- k_weight: bfloat16 [2048, 2048], P(None, 'tensor'), may hold values from -0.125 to 0.125
- v_weight: bfloat16 [2048, 2048], P(None, 'tensor'), may hold values from -0.125 to 0.125
- o_weight: bfloat16 [2048, 2048], P(None, 'tensor'), may hold values from -0.5 to 0.5
- norm2_gain: bfloat16 [2048], replicated, may hold values from 0.5 to 1.5
- router_weight: bfloat16 [2048, 8], replicated, may hold values from -0.0625 to 0.0625
- shared_gate_vector: bfloat16 [2048], replicated, may hold values from -0.125 to 0.125
- shared_gate_weight: bfloat16 [2048, 5632], P(None, 'tensor'), may hold values from -0.125 to 0.125
- shared_up_weight: bfloat16 [2048, 5632], P(None, 'tensor'), may hold values from -0.125 to 0.125
- shared_down_weight: bfloat16 [2048, 5632], P(None, 'tensor'), may hold values from -0.25 to 0.25
- expert_gate_weight: bfloat16 [8, 2048, 1408], P('expert', None, 'tensor'), may hold values from -0.125 to 0.125
- expert_up_weight: bfloat16 [8, 2048, 1408], P('expert', None, 'tensor'), may hold values from -0.125 to 0.125
- expert_down_weight: bfloat16 [8, 2048, 1408], P('expert', None, 'tensor'), may hold values from -1 to 1
- out_grad: bfloat16 [4096, 2048], P(('dp', 'expert')), may hold values from -6 to 6
Outputs:
- layer_out: float32 [4096, 2048], P(('dp', 'expert'))
- input_grad: float32 [4096, 2048], P(('dp', 'expert'))
- rms_stats: float32 [2, 4096], P(None, ('dp', 'expert'))
- norm1_gain_grad: float32 [2048], P(('dp', 'expert'))
- q_weight_grad: float32 [2048, 2048], P(('dp', 'expert'), 'tensor')
- k_weight_grad: float32 [2048, 2048], P(('dp', 'expert'), 'tensor')
- v_weight_grad: float32 [2048, 2048], P(('dp', 'expert'), 'tensor')
- o_weight_grad: float32 [2048, 2048], P(('dp', 'expert'), 'tensor')
- norm2_gain_grad: float32 [2048], P(('dp', 'expert'))
- router_grad: float32 [2048, 8], P(('dp', 'expert'))
- shared_vector_grad: float32 [2048], P(('dp', 'expert'))
- shared_gate_grad: float32 [2048, 5632], P(('dp', 'expert'), 'tensor')
- shared_up_grad: float32 [2048, 5632], P(('dp', 'expert'), 'tensor')
- shared_down_grad: float32 [2048, 5632], P(('dp', 'expert'), 'tensor')
- expert_gate_grad: float32 [8, 2048, 1408], P('expert', 'dp', 'tensor')
- expert_up_grad: float32 [8, 2048, 1408], P('expert', 'dp', 'tensor')
- expert_down_grad: float32 [8, 2048, 1408], P('expert', 'dp', 'tensor')
Inputs may be any that keep to these rules, and one draw needn't show every extreme that they name: `segments`: document numbers never fall along a sequence; each of the 8 documents of a sequence is present and holds 1 to 512 tokens, one exactly 512. `routes`: the 4 experts of a token differ. Among the 256 tokens of one index of dp and expert, no expert is named more than 192 times, a bound that some block reaches.
All inputs are finite; a program needn't handle non-finite values.
Results may differ from a plain program's by a relative error of at most 0.02.
Values may be sent and summed in bfloat16 or wider, within the bound.
A program may use at most 384 MiB of HBM per device.

v0:
```python
import jax
import jax.numpy as jnp
from jax import lax
from jax.sharding import PartitionSpec as P

HD = 128
epsilon = 1e-06
precise = lax.Precision.HIGHEST


def norm_forward(values, gain):
    inverse = lax.rsqrt(jnp.mean(values * values, axis=-1, keepdims=True) + epsilon)
    return (values * inverse * gain, inverse)


def norm_backward(values, inverse, gain, upstream):
    scaled = upstream * gain
    gain_grad = jnp.sum(upstream * values * inverse, axis=0)
    inner = jnp.mean(scaled * values, axis=-1, keepdims=True)
    return (inverse * scaled - values * inverse * inverse * inverse * inner, gain_grad)


def silu_slope(values):
    sigma = jax.nn.sigmoid(values)
    return sigma * (1.0 + values * (1.0 - sigma))


def cross_rows(left, right):
    return lax.dot_general(
        left, right, (((0,), (0,)), ((), ())), preferred_element_type=jnp.float32
    )


def cross_cols(left, right):
    return lax.dot_general(
        left, right, (((1,), (1,)), ((), ())), preferred_element_type=jnp.float32
    )


def plain_dot(left, right):
    return jnp.dot(left, right, preferred_element_type=jnp.float32)


def body(
    tokens,
    segments,
    routes,
    norm1_gain,
    q_weight,
    k_weight,
    v_weight,
    o_weight,
    norm2_gain,
    router_weight,
    shared_gate_vector,
    shared_gate_weight,
    shared_up_weight,
    shared_down_weight,
    expert_gate_weight,
    expert_up_weight,
    expert_down_weight,
    out_grad,
):
    tok_rows = tokens.shape[0]
    feat_width = tokens.shape[1]
    local_count = expert_gate_weight.shape[0]
    expert_count = local_count * lax.axis_size("expert")
    top_count = routes.shape[1]
    slot_count = 3 * tok_rows * top_count // (2 * expert_count)
    head_count = q_weight.shape[1] // HD
    score_scale = HD ** (-0.5)
    first_norm_gain = norm1_gain.astype(jnp.float32)
    second_norm_gain = norm2_gain.astype(jnp.float32)
    input_rows = tokens.astype(jnp.float32)
    normed_one, inverse_one = norm_forward(input_rows, first_norm_gain)
    normed_low = normed_one.astype(jnp.bfloat16)
    queries = plain_dot(normed_low, q_weight).astype(jnp.bfloat16)
    own_keys = plain_dot(normed_low, k_weight).astype(jnp.bfloat16)
    own_values = plain_dot(normed_low, v_weight).astype(jnp.bfloat16)
    labels = segments.astype(jnp.bfloat16)
    all_keys, all_values, key_labels = (
        lax.all_gather(own_keys, "expert", axis=0, tiled=True),
        lax.all_gather(own_values, "expert", axis=0, tiled=True),
        lax.all_gather(labels, "expert", axis=1, tiled=True),
    )
    key_span = all_keys.shape[0]
    query_pos = lax.axis_index("expert") * tok_rows + jnp.arange(tok_rows)
    key_pos = jnp.arange(key_span)
    allowed = (key_pos[None, :] <= query_pos[:, None]) & (
        key_labels[0][None, :] == labels[0][:, None]
    )
    query_heads = queries.reshape(tok_rows, head_count, HD)
    key_heads = all_keys.reshape(key_span, head_count, HD)
    value_heads = all_values.reshape(key_span, head_count, HD)

    def masked_scores():
        raw_scores = (
            jnp.einsum("qhd,khd->hqk", query_heads, key_heads, preferred_element_type=jnp.float32)
            * score_scale
        )
        return jnp.where(allowed[None], raw_scores, -jnp.inf)

    scores = masked_scores()
    top_score = jnp.max(scores, axis=-1, keepdims=True)
    exponent = jnp.exp(scores - top_score)
    totals = jnp.sum(exponent, axis=-1, keepdims=True)
    log_total = top_score + jnp.log(totals)
    weights_low = (exponent / totals).astype(jnp.bfloat16)
    mixed_heads = jnp.einsum(
        "hqk,khd->qhd", weights_low, value_heads, preferred_element_type=jnp.float32
    )
    mixed_low = mixed_heads.reshape(tok_rows, -1).astype(jnp.bfloat16)
    residual_state = input_rows + lax.psum(
        cross_cols(mixed_low, o_weight).astype(jnp.bfloat16), "tensor"
    ).astype(jnp.float32)
    normed_two, inverse_two = norm_forward(residual_state, second_norm_gain)
    routed_in = normed_two.astype(jnp.bfloat16)
    router_probs = jax.nn.softmax(plain_dot(routed_in, router_weight), axis=-1)
    chosen = routes[:, :, None] == jnp.arange(expert_count)[None, None, :]
    gate_values = jnp.sum(jnp.where(chosen, router_probs[:, None, :], 0.0), axis=-1)
    shared_gate_pre = plain_dot(routed_in, shared_gate_weight)
    shared_up_pre = plain_dot(routed_in, shared_up_weight)
    shared_hidden = (jax.nn.silu(shared_gate_pre) * shared_up_pre).astype(jnp.bfloat16)
    shared_out = cross_cols(shared_hidden, shared_down_weight)
    shared_sigma = jax.nn.sigmoid(plain_dot(routed_in, shared_gate_vector))
    flat_routes = routes.reshape(-1)
    route_hot = (flat_routes[:, None] == jnp.arange(expert_count)[None, :]).astype(jnp.int32)
    slot_index = jnp.sum((jnp.cumsum(route_hot, axis=0) - 1) * route_hot, axis=1)
    placement = flat_routes * slot_count + slot_index
    assign_total = tok_rows * top_count
    owners = (
        jnp.full((expert_count * slot_count,), assign_total, jnp.int32)
        .at[placement]
        .set(jnp.arange(assign_total, dtype=jnp.int32))
    )
    padded_rows = jnp.concatenate([routed_in, jnp.zeros((1, feat_width), jnp.bfloat16)], axis=0)
    outgoing = padded_rows[owners // top_count].reshape(expert_count, 1, slot_count, feat_width)
    received = lax.all_to_all(outgoing, "expert", split_axis=0, concat_axis=1, tiled=True)
    gate_pre = jnp.einsum(
        "esmd,edf->esmf", received, expert_gate_weight, preferred_element_type=jnp.float32
    )
    up_pre = jnp.einsum(
        "esmd,edf->esmf", received, expert_up_weight, preferred_element_type=jnp.float32
    )
    expert_hidden = (jax.nn.silu(gate_pre) * up_pre).astype(jnp.bfloat16)
    result = jnp.einsum(
        "esmf,edf->esmd", expert_hidden, expert_down_weight, preferred_element_type=jnp.float32
    )
    returned = lax.all_to_all(
        result.astype(jnp.bfloat16), "expert", split_axis=1, concat_axis=0, tiled=True
    ).astype(result.dtype)
    picked = returned.reshape(expert_count * slot_count, feat_width)[placement].reshape(
        tok_rows, top_count, feat_width
    )
    routed_output = jnp.sum(gate_values[:, :, None] * picked, axis=1)
    branch_sum = lax.psum(
        (routed_output + shared_sigma[:, None] * shared_out).astype(jnp.bfloat16), "tensor"
    ).astype(jnp.float32)
    layer_out = residual_state + branch_sum
    upstream = out_grad.astype(jnp.float32)
    d_shared = (shared_sigma[:, None] * upstream).astype(jnp.bfloat16)
    d_sigma = jnp.sum(upstream * shared_out, axis=-1)
    d_shared_hidden = plain_dot(d_shared, shared_down_weight)
    d_shared_gate = (d_shared_hidden * shared_up_pre * silu_slope(shared_gate_pre)).astype(
        jnp.bfloat16
    )
    d_shared_up = (d_shared_hidden * jax.nn.silu(shared_gate_pre)).astype(jnp.bfloat16)
    grad_shared_gate = cross_rows(routed_in, d_shared_gate)
    grad_shared_up = cross_rows(routed_in, d_shared_up)
    grad_shared_down = cross_rows(d_shared, shared_hidden)
    d_routed = cross_cols(d_shared_gate, shared_gate_weight) + cross_cols(
        d_shared_up, shared_up_weight
    )
    d_gates = jnp.sum(upstream[:, None, :] * picked, axis=-1)
    d_expert_out = (
        (gate_values[:, :, None] * upstream[:, None, :])
        .astype(jnp.bfloat16)
        .reshape(assign_total, feat_width)
    )
    padded_grads = jnp.concatenate([d_expert_out, jnp.zeros((1, feat_width), jnp.bfloat16)], axis=0)
    grads_out = padded_grads[owners].reshape(expert_count, 1, slot_count, feat_width)
    incoming = lax.all_to_all(grads_out, "expert", split_axis=0, concat_axis=1, tiled=True)
    expert_hidden = (jax.nn.silu(gate_pre) * up_pre).astype(jnp.bfloat16)
    d_hidden = jnp.einsum(
        "esmd,edf->esmf", incoming, expert_down_weight, preferred_element_type=jnp.float32
    )
    d_gate_pre = (d_hidden * up_pre * silu_slope(gate_pre)).astype(jnp.bfloat16)
    d_up_pre = (d_hidden * jax.nn.silu(gate_pre)).astype(jnp.bfloat16)
    d_rows = jnp.einsum(
        "esmf,edf->esmd", d_gate_pre, expert_gate_weight, preferred_element_type=jnp.float32
    )
    d_rows = d_rows + jnp.einsum(
        "esmf,edf->esmd", d_up_pre, expert_up_weight, preferred_element_type=jnp.float32
    )
    d_back = lax.all_to_all(
        d_rows.astype(jnp.bfloat16), "expert", split_axis=1, concat_axis=0, tiled=True
    ).astype(d_rows.dtype)
    grad_expert_gate = jnp.einsum(
        "esmd,esmf->edf", received, d_gate_pre, preferred_element_type=jnp.float32
    )
    grad_expert_up = jnp.einsum(
        "esmd,esmf->edf", received, d_up_pre, preferred_element_type=jnp.float32
    )
    grad_expert_down = jnp.einsum(
        "esmd,esmf->edf", incoming, expert_hidden, preferred_element_type=jnp.float32
    )
    sum_gate, sum_up, sum_down = (
        lax.psum_scatter(
            grad_expert_gate.astype(jnp.bfloat16), "dp", scatter_dimension=1, tiled=True
        ).astype(jnp.float32),
        lax.psum_scatter(
            grad_expert_up.astype(jnp.bfloat16), "dp", scatter_dimension=1, tiled=True
        ).astype(jnp.float32),
        lax.psum_scatter(
            grad_expert_down.astype(jnp.bfloat16), "dp", scatter_dimension=1, tiled=True
        ).astype(jnp.float32),
    )
    back_rows = d_back.reshape(expert_count * slot_count, feat_width)[placement].reshape(
        tok_rows, top_count, feat_width
    )
    d_routed = d_routed + jnp.sum(back_rows, axis=1)
    d_probs = jnp.sum(jnp.where(chosen, d_gates[:, :, None], 0.0), axis=1)
    d_logits = router_probs * (d_probs - jnp.sum(router_probs * d_probs, axis=-1, keepdims=True))
    d_vector = d_sigma * shared_sigma * (1.0 - shared_sigma)
    router_matrix = router_weight.astype(jnp.float32)
    gate_vector_weight = shared_gate_vector.astype(jnp.float32)
    d_routed = (
        d_routed
        + jnp.dot(d_logits, router_matrix.T, precision=precise)
        + d_vector[:, None] * gate_vector_weight[None, :]
    )
    d_normed_two, d_logits, d_vector = (
        lax.psum(d_routed.astype(jnp.bfloat16), "tensor").astype(jnp.float32),
        lax.psum(d_logits.astype(jnp.bfloat16), "tensor").astype(jnp.float32),
        lax.psum(d_vector.astype(jnp.bfloat16), "tensor").astype(jnp.float32),
    )
    grad_router = jnp.dot(
        routed_in.T, d_logits, precision=precise, preferred_element_type=jnp.float32
    )
    grad_vector = jnp.dot(
        routed_in.T, d_vector, precision=precise, preferred_element_type=jnp.float32
    )
    d_hidden_norm, grad_norm_two = norm_backward(
        residual_state, inverse_two, second_norm_gain, d_normed_two
    )
    d_state = upstream + d_hidden_norm
    d_state_low = d_state.astype(jnp.bfloat16)
    d_mixed = plain_dot(d_state_low, o_weight).astype(jnp.bfloat16)
    grad_out_proj = cross_rows(d_state_low, mixed_low)
    probs_full = jnp.exp(masked_scores() - log_total)
    probs_low = probs_full.astype(jnp.bfloat16)
    d_mixed_heads = d_mixed.reshape(tok_rows, head_count, HD)
    d_value_all = jnp.einsum(
        "hqk,qhd->khd", probs_low, d_mixed_heads, preferred_element_type=jnp.float32
    )
    d_probs_att = jnp.einsum(
        "qhd,khd->hqk", d_mixed_heads, value_heads, preferred_element_type=jnp.float32
    )
    d_scores = (
        probs_full * (d_probs_att - jnp.sum(probs_full * d_probs_att, axis=-1, keepdims=True))
    ).astype(jnp.bfloat16)
    d_queries = (
        (
            jnp.einsum("hqk,khd->qhd", d_scores, key_heads, preferred_element_type=jnp.float32)
            * score_scale
        )
        .reshape(tok_rows, -1)
        .astype(jnp.bfloat16)
    )
    d_key_all = (
        jnp.einsum("hqk,qhd->khd", d_scores, query_heads, preferred_element_type=jnp.float32)
        * score_scale
    )
    d_keys, d_values = (
        lax.psum_scatter(
            d_key_all.reshape(key_span, -1).astype(jnp.bfloat16),
            "expert",
            scatter_dimension=0,
            tiled=True,
        ).astype(jnp.float32),
        lax.psum_scatter(
            d_value_all.reshape(key_span, -1).astype(jnp.bfloat16),
            "expert",
            scatter_dimension=0,
            tiled=True,
        ).astype(jnp.float32),
    )
    d_keys_low = d_keys.astype(jnp.bfloat16)
    d_values_low = d_values.astype(jnp.bfloat16)
    grad_query = cross_rows(normed_low, d_queries)
    grad_key = cross_rows(normed_low, d_keys_low)
    grad_value = cross_rows(normed_low, d_values_low)
    d_normed_one = (
        cross_cols(d_queries, q_weight)
        + cross_cols(d_keys_low, k_weight)
        + cross_cols(d_values_low, v_weight)
    )
    d_normed_one = lax.psum(d_normed_one.astype(jnp.bfloat16), "tensor").astype(jnp.float32)
    d_input_norm, grad_norm_one = norm_backward(
        input_rows, inverse_one, first_norm_gain, d_normed_one
    )
    input_grad = d_state + d_input_norm
    stats = jnp.concatenate([inverse_one.T, inverse_two.T], axis=0)
    g_one, g_query, g_key, g_value, g_out, g_two, g_router, g_vector, g_sgate, g_sup, g_sdown = (
        lax.psum_scatter(grad_norm_one, ("dp", "expert"), scatter_dimension=0, tiled=True),
        lax.psum_scatter(grad_query, ("dp", "expert"), scatter_dimension=0, tiled=True),
        lax.psum_scatter(grad_key, ("dp", "expert"), scatter_dimension=0, tiled=True),
        lax.psum_scatter(grad_value, ("dp", "expert"), scatter_dimension=0, tiled=True),
        lax.psum_scatter(grad_out_proj, ("dp", "expert"), scatter_dimension=0, tiled=True),
        lax.psum_scatter(grad_norm_two, ("dp", "expert"), scatter_dimension=0, tiled=True),
        lax.psum_scatter(grad_router, ("dp", "expert"), scatter_dimension=0, tiled=True),
        lax.psum_scatter(grad_vector, ("dp", "expert"), scatter_dimension=0, tiled=True),
        lax.psum_scatter(grad_shared_gate, ("dp", "expert"), scatter_dimension=0, tiled=True),
        lax.psum_scatter(grad_shared_up, ("dp", "expert"), scatter_dimension=0, tiled=True),
        lax.psum_scatter(grad_shared_down, ("dp", "expert"), scatter_dimension=0, tiled=True),
    )
    return (
        layer_out,
        input_grad,
        stats,
        g_one,
        g_query,
        g_key,
        g_value,
        g_out,
        g_two,
        g_router,
        g_vector,
        g_sgate,
        g_sup,
        g_sdown,
        sum_gate,
        sum_up,
        sum_down,
    )


def solution(mesh):
    placed = (
        P(("dp", "expert"), None),
        P("dp", "expert"),
        P(("dp", "expert"), None),
        P(),
        P(None, "tensor"),
        P(None, "tensor"),
        P(None, "tensor"),
        P(None, "tensor"),
        P(),
        P(),
        P(),
        P(None, "tensor"),
        P(None, "tensor"),
        P(None, "tensor"),
        P("expert", None, "tensor"),
        P("expert", None, "tensor"),
        P("expert", None, "tensor"),
        P(("dp", "expert"), None),
    )
    return jax.shard_map(
        body,
        mesh=mesh,
        in_specs=placed,
        out_specs=(
            P(("dp", "expert"), None),
            P(("dp", "expert"), None),
            P(None, ("dp", "expert")),
            P(("dp", "expert")),
            P(("dp", "expert"), "tensor"),
            P(("dp", "expert"), "tensor"),
            P(("dp", "expert"), "tensor"),
            P(("dp", "expert"), "tensor"),
            P(("dp", "expert")),
            P(("dp", "expert"), None),
            P(("dp", "expert")),
            P(("dp", "expert"), "tensor"),
            P(("dp", "expert"), "tensor"),
            P(("dp", "expert"), "tensor"),
            P("expert", "dp", "tensor"),
            P("expert", "dp", "tensor"),
            P("expert", "dp", "tensor"),
        ),
        check_vma=False,
    )
```

profile of v0, /device:TPU:0, one launch (start us, length us, event | category | flops | bytes accessed | tf_op | source)
XLA Modules:
  0.0 3415.2 jit_solution(6877648826485437788)
XLA Ops:
  23.5 12.7 all_gather.12
  37.2 25.9 all-gather.5.cloned.1.call-done
  74.6 35.3 %all-gather.3.cloned.1.call-done = bf16[1024,1024]{1,0:T(8,128)(2,1)} async-done(((bf16[256,1024]{1,0:T(8,128)(2,1)}), bf16[1024,1024]{1,0:T(8,128)(2,1)}) %all-gather.3.cloned.1.call-update) | async-done | bytes 2097168 | tf_op jit(solution)/shard_map/all_gather | solution.py:83
  126.6 10.4 all-reduce.12.cloned.1.call-done
  141.0 7.1 gather_fusion
  158.9 10.0 mul.339
  177.0 15.4 gather_fusion.2
  192.5 100.0 %all-to-all-done = bf16[8,1,192,2048]{3,2,1,0:T(8,128)(2,1)} async-done(((bf16[8,1,192,2048]{3,2,1,0:T(8,128)(2,1)}), bf16[8,1,192,2048]{3,2,1,0:T(8,128)(2,1)}, u32[]{:S(2)}, u32[]{:S(2)}) %all-to-all-start) | async-done | bytes 6291488 | tf_op jit(solution)/shard_map/all_to_all | solution.py:138
  297.9 10.3 fusion.6
  308.2 127.8 %all-to-all-done.2 = bf16[8,1,192,2048]{3,2,1,0:T(8,128)(2,1)} async-done(((bf16[8,1,192,2048]{3,2,1,0:T(8,128)(2,1)}), bf16[8,1,192,2048]{3,2,1,0:T(8,128)(2,1)}, u32[]{:S(2)}, u32[]{:S(2)}) %all-to-all-start.2) | async-done | bytes 6291488 | tf_op jit(solution)/shard_map/all_to_all | solution.py:182
  436.0 11.0 fusion.4
  446.9 13.4 multiply_convert_fusion.3
  474.7 11.0 fusion.11
  485.7 10.0 add_convert_fusion
  498.9 113.4 %all-to-all-done.1 = bf16[2,4,192,2048]{3,2,0,1:T(8,128)(2,1)} async-done(((bf16[2,4,192,2048]{3,2,0,1:T(8,128)(2,1)}), bf16[2,4,192,2048]{3,2,0,1:T(8,128)(2,1)}, u32[]{:S(2)}, u32[]{:S(2)}) %all-to-all-start.1) | async-done | bytes 6291488 | tf_op jit(solution)/shard_map/all_to_all | solution.py:149
  626.1 10.3 multiply_convert_fusion.8
  641.4 7.2 multiply_convert_fusion.6
  648.6 9.3 fusion.112
  657.9 8.8 bitcast_convert_fusion.4
  666.7 13.7 gather_fusion.1
  680.5 10.0 reshape.289
  690.5 11.1 multiply_reduce_fusion.1
  701.8 53.4 %all-to-all-done.3 = bf16[2,4,192,2048]{3,2,0,1:T(8,128)(2,1)} async-done(((bf16[2,4,192,2048]{3,2,0,1:T(8,128)(2,1)}), bf16[2,4,192,2048]{3,2,0,1:T(8,128)(2,1)}, u32[]{:S(2)}, u32[]{:S(2)}) %all-to-all-start.3) | async-done | bytes 6291488 | tf_op jit(solution)/shard_map/all_to_all | solution.py:195
  755.2 8.8 bitcast_convert_fusion.3
  764.0 13.6 gather_fusion.3
  777.6 9.8 reshape.291
  787.4 8.6 reduce_sum.163
  796.1 8.5 fusion.44
  806.9 18.9 all-reduce.14.cloned.1.call-done
  851.3 11.0 bitcast_convert_fusion
  862.8 10.7 bitcast_convert_fusion.2
  873.6 10.7 bitcast_convert_fusion.1
  899.7 36.4 %reduce-scatter.16.cloned.1.call-done = bf16[256,1024]{0,1:T(8,128)(2,1)} async-done(((bf16[1024,1024]{0,1:T(8,128)(2,1)}), bf16[256,1024]{0,1:T(8,128)(2,1)}) %reduce-scatter.16.cloned.1.call-update) | async-done | bytes 524304 | tf_op jit(solution)/shard_map/reduce_scatter | solution.py:281
  944.9 7.4 fusion.81
  970.8 11.0 fusion.84
  981.9 10.8 fusion.116
  992.8 10.9 fusion.115
  1009.7 63.3 %reduce-scatter.34.cloned.1.call-done = bf16[2,512,704]{1,2,0:T(8,128)(2,1)} async-done(((bf16[2,2048,704]{1,2,0:T(8,128)(2,1)}), bf16[2,512,704]{1,2,0:T(8,128)(2,1)}) %reduce-scatter.34.cloned.1.call-update) | async-done | bytes 1441808 | tf_op jit(solution)/shard_map/reduce_scatter | solution.py:208
  1076.4 65.5 %reduce-scatter.36.cloned.1.call-done = bf16[2,512,704]{1,2,0:T(8,128)(2,1)} async-done(((bf16[2,2048,704]{1,2,0:T(8,128)(2,1)}), bf16[2,512,704]{1,2,0:T(8,128)(2,1)}) %reduce-scatter.36.cloned.1.call-update) | async-done | bytes 1441808 | tf_op jit(solution)/shard_map/reduce_scatter | solution.py:211
  1145.2 20.8 all-reduce.16.cloned.1.call-done
  1167.9 77.4 %all-reduce.5 = (f32[2048]{0:T(1024)S(1)}, f32[2048]{0:T(1024)S(1)}, f32[2048]{0:T(1024)S(1)}) all-reduce(f32[2048]{0:T(1024)S(1)} %get-tuple-element.21, f32[2048]{0:T(1024)S(1)} %get-tuple-element.19, f32[2048]{0:T(1024)S(1)} %bitcast.206), channel_id=4, replica_groups=mesh['dp'=4,'expert'=4,'tensor'=2] {'dp','expert'}, use_global_device_ids=true, to_apply=%region_27.28.clone | all-reduce | flops 6144 | bytes 49152
  1252.8 174.7 %reduce-scatter.24.cloned.1.call-done = f32[128,1024]{1,0:T(8,128)} async-done(((f32[2048,1024]{1,0:T(8,128)}), f32[128,1024]{1,0:T(8,128)}) %reduce-scatter.24.cloned.1.call-update) | async-done | bytes 524304 | tf_op jit(solution)/shard_map/reduce_scatter | solution.py:309
  1427.5 182.7 %reduce-scatter.18.cloned.1.call-done = f32[128,1024]{1,0:T(8,128)} async-done(((f32[2048,1024]{1,0:T(8,128)}), f32[128,1024]{1,0:T(8,128)}) %reduce-scatter.18.cloned.1.call-update) | async-done | bytes 524304 | tf_op jit(solution)/shard_map/reduce_scatter | solution.py:306
  1610.2 182.6 %reduce-scatter.22.cloned.1.call-done = f32[128,1024]{1,0:T(8,128)} async-done(((f32[2048,1024]{1,0:T(8,128)}), f32[128,1024]{1,0:T(8,128)}) %reduce-scatter.22.cloned.1.call-update) | async-done | bytes 524304 | tf_op jit(solution)/shard_map/reduce_scatter | solution.py:308
  1792.8 182.6 %reduce-scatter.20.cloned.1.call-done = f32[128,1024]{1,0:T(8,128)} async-done(((f32[2048,1024]{1,0:T(8,128)}), f32[128,1024]{1,0:T(8,128)}) %reduce-scatter.20.cloned.1.call-update) | async-done | bytes 524304 | tf_op jit(solution)/shard_map/reduce_scatter | solution.py:307
  1975.4 476.0 %reduce-scatter.32.cloned.1.call-done = f32[128,2816]{1,0:T(8,128)} async-done(((f32[2048,2816]{1,0:T(8,128)}), f32[128,2816]{1,0:T(8,128)}) %reduce-scatter.32.cloned.1.call-update) | async-done | bytes 1441808 | tf_op jit(solution)/shard_map/reduce_scatter | solution.py:315
  2451.3 478.4 %reduce-scatter.30.cloned.1.call-done = f32[128,2816]{1,0:T(8,128)} async-done(((f32[2048,2816]{1,0:T(8,128)}), f32[128,2816]{1,0:T(8,128)}) %reduce-scatter.30.cloned.1.call-update) | async-done | bytes 1441808 | tf_op jit(solution)/shard_map/reduce_scatter | solution.py:314
  2929.8 478.4 %reduce-scatter.28.cloned.1.call-done = f32[128,2816]{1,0:T(8,128)} async-done(((f32[2048,2816]{1,0:T(8,128)}), f32[128,2816]{1,0:T(8,128)}) %reduce-scatter.28.cloned.1.call-update) | async-done | bytes 1441808 | tf_op jit(solution)/shard_map/reduce_scatter | solution.py:313
  (263 shorter events, 202.2 us)
Async XLA Ops:
  7.2 161.7 %copy-start = (bf16[2048,8]{0,1:T(8,128)(2,1)S(1)}, bf16[2048,8]{0,1:T(8,128)(2,1)}, u32[]{:S(2)}) copy-start(bf16[2048,8]{0,1:T(8,128)(2,1)} %param.27) | copy-start | bytes 98308
  7.2 55.9 %all-gather.5.cloned.1.call-start = ((), (), s32[]{:S(2)}) async-start(), calls=%async_computation.18 | async-start | bytes 2621440 | tf_op jit(solution)/shard_map/all_gather | solution.py:82
  8.8 10.2 copy-start.27
  14.2 95.7 %all-gather.3.cloned.1.call-start = ((), (), s32[]{:S(2)}) async-start(), calls=%async_computation.17 | async-start | bytes 2621440 | tf_op jit(solution)/shard_map/all_gather | solution.py:83
  18.6 118.3 %all-reduce.12.cloned.1.call-start = ((), (), s32[]{:S(2)}) async-start(), calls=%async_computation.19 | async-start | bytes 2097152 | tf_op jit(solution)/shard_map/psum | solution.py:113
  69.4 40.5 %copy-start.31 = (f32[8,256]{1,0:T(8,128)}, f32[8,256]{1,0:T(8,128)S(1)}, u32[]{:S(2)}) copy-start(f32[8,256]{1,0:T(8,128)S(1)} %get-tuple-element.42) | copy-start | bytes 24580
  74.6 41.5 %copy-start.37 = (f32[8,256]{1,0:T(8,128)}, f32[8,256]{1,0:T(8,128)S(1)}, u32[]{:S(2)}) copy-start(f32[8,256]{1,0:T(8,128)S(1)} %fusion) | copy-start | bytes 24580
  118.6 22.3 copy-start.23
  140.9 485.1 %copy-start.4 = (bf16[256,2048]{1,0:T(8,128)(2,1)}, bf16[256,2048]{1,0:T(8,128)(2,1)S(1)}, u32[]{:S(2)}) copy-start(bf16[256,2048]{1,0:T(8,128)(2,1)S(1)} %multiply_convert_fusion.10) | copy-start | bytes 3145732
  148.1 144.3 %all-to-all-start = ((bf16[8,1,192,2048]{3,2,1,0:T(8,128)(2,1)}), bf16[8,1,192,2048]{3,2,1,0:T(8,128)(2,1)}, u32[]{:S(2)}, u32[]{:S(2)}) async-start(bf16[8,1,192,2048]{3,2,1,0:T(8,128)(2,1)} %bitcast.190), calls=%async_computation | async-start | bytes 12582912 | tf_op jit(solution)/shard_map/all_to_all | solution.py:138
  292.4 143.6 %all-to-all-start.2 = ((bf16[8,1,192,2048]{3,2,1,0:T(8,128)(2,1)}), bf16[8,1,192,2048]{3,2,1,0:T(8,128)(2,1)}, u32[]{:S(2)}, u32[]{:S(2)}) async-start(bf16[8,1,192,2048]{3,2,1,0:T(8,128)(2,1)} %bitcast.191), calls=%async_computation.2 | async-start | bytes 12582912 | tf_op jit(solution)/shard_map/all_to_all | solution.py:182
  436.0 24.4 slice-start.5
  446.9 13.4 slice-start.6
  469.0 143.3 %all-to-all-start.1 = ((bf16[2,4,192,2048]{3,2,0,1:T(8,128)(2,1)}), bf16[2,4,192,2048]{3,2,0,1:T(8,128)(2,1)}, u32[]{:S(2)}, u32[]{:S(2)}) async-start(bf16[2,4,192,2048]{3,2,0,1:T(8,128)(2,1)} %copy.121), calls=%async_computation.1 | async-start | bytes 12582912 | tf_op jit(solution)/shard_map/all_to_all | solution.py:149
  474.7 11.0 copy-start.51
  498.9 118.7 %copy-start.41 = (bf16[2048]{0:T(1024)(128)(2,1)S(1)}, bf16[2048]{0:T(1024)(128)(2,1)}, u32[]{:S(2)}) copy-start(bf16[2048]{0:T(1024)(128)(2,1)} %param.28) | copy-start | bytes 12292
  612.3 142.9 %all-to-all-start.3 = ((bf16[2,4,192,2048]{3,2,0,1:T(8,128)(2,1)}), bf16[2,4,192,2048]{3,2,0,1:T(8,128)(2,1)}, u32[]{:S(2)}, u32[]{:S(2)}) async-start(bf16[2,4,192,2048]{3,2,0,1:T(8,128)(2,1)} %copy.125), calls=%async_computation.3 | async-start | bytes 12582912 | tf_op jit(solution)/shard_map/all_to_all | solution.py:195
  617.6 208.2 %all-reduce.14.cloned.1.call-start = ((), (), s32[]{:S(2)}) async-start(), calls=%async_computation.20 | async-start | bytes 2097152 | tf_op jit(solution)/shard_map/psum | solution.py:233
  619.6 16.8 slice-start.2
  619.6 16.8 slice-start.3
  626.0 10.3 copy-start.50
  626.0 10.3 slice-start.4
  680.5 10.0 copy-start.21
  690.5 11.2 copy-start.34
  690.5 11.3 copy-start.26
  690.5 11.3 copy-start.40
  690.5 11.2 copy-start.43
  804.6 21.2 copy-start.3
  804.6 21.2 copy-start.9
  804.6 21.2 copy-start.24
  804.6 21.2 copy-start.36
  806.8 87.3 %reduce-scatter.14.cloned.1.call-start = ((), (), s32[]{:S(2)}) async-start(), calls=%async_computation.21 | async-start | bytes 2621440 | tf_op jit(solution)/shard_map/reduce_scatter | solution.py:275
  844.8 91.2 %reduce-scatter.16.cloned.1.call-start = ((), (), s32[]{:S(2)}) async-start(), calls=%async_computation.22 | async-start | bytes 2621440 | tf_op jit(solution)/shard_map/reduce_scatter | solution.py:281
  851.2 155.2 %reduce-scatter.38.cloned.1.call-start = ((), (), s32[]{:S(2)}) async-start(), calls=%async_computation.33 | async-start | bytes 7208960 | tf_op jit(solution)/shard_map/reduce_scatter | solution.py:214
  862.3 210.7 %reduce-scatter.34.cloned.1.call-start = ((), (), s32[]{:S(2)}) async-start(), calls=%async_computation.31 | async-start | bytes 7208960 | tf_op jit(solution)/shard_map/reduce_scatter | solution.py:208
  873.5 268.4 %reduce-scatter.36.cloned.1.call-start = ((), (), s32[]{:S(2)}) async-start(), calls=%async_computation.32 | async-start | bytes 7208960 | tf_op jit(solution)/shard_map/reduce_scatter | solution.py:211
  884.3 281.7 %all-reduce.16.cloned.1.call-start = ((), (), s32[]{:S(2)}) async-start(), calls=%async_computation.34 | async-start | bytes 4194304 | tf_op jit(solution)/shard_map/psum | solution.py:156
  899.7 41.8 %copy-start.45 = (bf16[256]{0:T(256)(128)(2,1)S(1)}, bf16[256]{0:T(256)(128)(2,1)}, u32[]{:S(2)}) copy-start(bf16[256]{0:T(256)(128)(2,1)} %get-tuple-element.30) | copy-start | bytes 1540
  899.7 44.3 %copy-start.5 = (bf16[256,2048]{1,0:T(8,128)(2,1)S(1)}, bf16[256,2048]{1,0:T(8,128)(2,1)}, u32[]{:S(2)}) copy-start(bf16[256,2048]{1,0:T(8,128)(2,1)} %copy-done.4) | copy-start | bytes 3145732
  941.4 311.4 %reduce-scatter.26.cloned.1.call-start = ((), (), s32[]{:S(2)}) async-start(), calls=%async_computation.27 | async-start | bytes 69632 | tf_op jit(solution)/shard_map/reduce_scatter | solution.py:311
  944.9 482.6 %reduce-scatter.24.cloned.1.call-start = ((), (), s32[]{:S(2)}) async-start(), calls=%async_computation.26 | async-start | bytes 8912896 | tf_op jit(solution)/shard_map/reduce_scatter | solution.py:309
  952.3 657.9 %reduce-scatter.18.cloned.1.call-start = ((), (), s32[]{:S(2)}) async-start(), calls=%async_computation.23 | async-start | bytes 8912896 | tf_op jit(solution)/shard_map/reduce_scatter | solution.py:306
  958.9 833.9 %reduce-scatter.22.cloned.1.call-start = ((), (), s32[]{:S(2)}) async-start(), calls=%async_computation.25 | async-start | bytes 8912896 | tf_op jit(solution)/shard_map/reduce_scatter | solution.py:308
  964.7 1010.6 %reduce-scatter.20.cloned.1.call-start = ((), (), s32[]{:S(2)}) async-start(), calls=%async_computation.24 | async-start | bytes 8912896 | tf_op jit(solution)/shard_map/reduce_scatter | solution.py:307
  970.6 1480.8 %reduce-scatter.32.cloned.1.call-start = ((), (), s32[]{:S(2)}) async-start(), calls=%async_computation.30 | async-start | bytes 24510464 | tf_op jit(solution)/shard_map/reduce_scatter | solution.py:315
  981.9 1947.9 %reduce-scatter.30.cloned.1.call-start = ((), (), s32[]{:S(2)}) async-start(), calls=%async_computation.29 | async-start | bytes 24510464 | tf_op jit(solution)/shard_map/reduce_scatter | solution.py:314
  992.7 2415.5 %reduce-scatter.28.cloned.1.call-start = ((), (), s32[]{:S(2)}) async-start(), calls=%async_computation.28 | async-start | bytes 24510464 | tf_op jit(solution)/shard_map/reduce_scatter | solution.py:313
  1076.4 170.6 %copy-start.10 = (bf16[256,2048]{1,0:T(8,128)(2,1)S(1)}, bf16[256,2048]{1,0:T(8,128)(2,1)}, u32[]{:S(2)}) copy-start(bf16[256,2048]{1,0:T(8,128)(2,1)} %all-reduce.12.cloned.1.call-done) | copy-start | bytes 3145732
  (34 other events, 131.6 us)
Sparse Core Ops, SparseCore 0:
  14.3 48.7 all-gather.4
  65.2 44.6 all-gather.2
  118.6 18.3 all-reduce.11
  806.9 18.8 all-reduce.13
  844.9 45.0 reduce-scatter.13
  892.9 43.1 reduce-scatter.15
  939.1 65.1 reduce-scatter.37
  1007.2 65.8 reduce-scatter.33
  1076.1 65.8 reduce-scatter.35
  1144.7 21.2 all-reduce.15
  1168.9 76.9 reduce-scatter.25
  1248.7 178.8 reduce-scatter.23
  1430.4 179.8 reduce-scatter.17
  1613.0 179.8 reduce-scatter.21
  1795.5 179.8 reduce-scatter.19
  1978.1 473.1 reduce-scatter.31
  2454.1 475.6 reduce-scatter.29
  2932.5 475.6 reduce-scatter.27
where the time goes:
time: 3430 us; the launch traced here: 3420 us
  waiting for transfers between devices  2830 us (83%)
  matrix products  262 us (8%)
  local copies, waits for them, and re-layouts  114 us (3%)
  blocking collectives  92.6 us (3%)
  other arithmetic  80.3 us (2%)
    reduce_scatter x1, waiting for transfers between devices, body(): lax.psum_scatter(grad_shared_gate, ('dp', 'expert'), scatter_dimension=0,...  478 us
    reduce_scatter x1, waiting for transfers between devices, body(): lax.psum_scatter(grad_shared_up, ('dp', 'expert'), scatter_dimension=0, t...  478 us
    reduce_scatter x1, waiting for transfers between devices, body(): lax.psum_scatter(grad_shared_down, ('dp', 'expert'), scatter_dimension=0,...  476 us
    reduce_scatter x1, waiting for transfers between devices, body(): lax.psum_scatter(grad_query, ('dp', 'expert'), scatter_dimension=0, tiled...  183 us
    reduce_scatter x1, waiting for transfers between devices, body(): lax.psum_scatter(grad_value, ('dp', 'expert'), scatter_dimension=0, tiled...  183 us
    reduce_scatter x1, waiting for transfers between devices, body(): lax.psum_scatter(grad_key, ('dp', 'expert'), scatter_dimension=0, tiled=T...  183 us
    reduce_scatter x1, waiting for transfers between devices, body(): lax.psum_scatter(grad_out_proj, ('dp', 'expert'), scatter_dimension=0, ti...  175 us
    all_to_all x1, waiting for transfers between devices, body(): lax.all_to_all(grads_out, 'expert', split_axis=0, concat_axis=1, tiled=True)  128 us
  transfers between devices with their start and end apart: 22, of which 19 were waited for; matrix products, arithmetic and copies ran while one was open for 9% of the time, Pallas kernels for 0%

commit v1 on v0

--- a/solution.py
+++ b/solution.py
@@ -2,6 +2,7 @@
 import jax.numpy as jnp
 from jax import lax
 from jax.sharding import PartitionSpec as P
+from jax.lax import all_to_all, axis_size
 
 HD = 128
 epsilon = 1e-06
@@ -146,9 +147,11 @@
     result = jnp.einsum(
         "esmf,edf->esmd", expert_hidden, expert_down_weight, preferred_element_type=jnp.float32
     )
-    returned = lax.all_to_all(
-        result.astype(jnp.bfloat16), "expert", split_axis=1, concat_axis=0, tiled=True
-    ).astype(result.dtype)
+    links_carry = lambda mine, comm_axis, on_dim, at_axis: jnp.concatenate(
+        all_to_all(jnp.stack(jnp.split(mine, axis_size(comm_axis), axis=on_dim)), comm_axis, 0, 0),
+        axis=at_axis,
+    )
+    returned = links_carry(result.astype(jnp.bfloat16), "expert", 1, 0).astype(result.dtype)
     picked = returned.reshape(expert_count * slot_count, feat_width)[placement].reshape(
         tok_rows, top_count, feat_width
     )

time: 3430 us -> 3430 us (level)
  no operation moved by 1% of the time
where the time goes in v1:
time: 3430 us; the launch traced here: 3420 us
  waiting for transfers between devices  2830 us (83%)
  matrix products  262 us (8%)
  local copies, waits for them, and re-layouts  112 us (3%)
  blocking collectives  92.6 us (3%)
  other arithmetic  83.5 us (2%)
    reduce_scatter x1, waiting for transfers between devices, body(): lax.psum_scatter(grad_shared_gate, ('dp', 'expert'), scatter_dimension=0,...  478 us
    reduce_scatter x1, waiting for transfers between devices, body(): lax.psum_scatter(grad_shared_up, ('dp', 'expert'), scatter_dimension=0, t...  478 us
    reduce_scatter x1, waiting for transfers between devices, body(): lax.psum_scatter(grad_shared_down, ('dp', 'expert'), scatter_dimension=0,...  476 us
    reduce_scatter x1, waiting for transfers between devices, body(): lax.psum_scatter(grad_query, ('dp', 'expert'), scatter_dimension=0, tiled...  183 us
    reduce_scatter x1, waiting for transfers between devices, body(): lax.psum_scatter(grad_value, ('dp', 'expert'), scatter_dimension=0, tiled...  183 us
    reduce_scatter x1, waiting for transfers between devices, body(): lax.psum_scatter(grad_key, ('dp', 'expert'), scatter_dimension=0, tiled=T...  183 us
    reduce_scatter x1, waiting for transfers between devices, body(): lax.psum_scatter(grad_out_proj, ('dp', 'expert'), scatter_dimension=0, ti...  175 us
    all_to_all x1, waiting for transfers between devices, body(): lax.all_to_all(grads_out, 'expert', split_axis=0, concat_axis=1, tiled=True)  128 us
  transfers between devices with their start and end apart: 22, of which 19 were waited for; matrix products, arithmetic and copies ran while one was open for 9% of the time, Pallas kernels for 0%

profile of v1, /device:TPU:0, one launch (start us, length us, event | category | flops | bytes accessed | tf_op | source)
XLA Modules:
  0.0 3416.4 jit_solution(10644620796815329896)
XLA Ops:
  23.5 12.7 all_gather.12
  37.2 25.9 all-gather.5.cloned.1.call-done
  74.6 35.3 %all-gather.3.cloned.1.call-done = bf16[1024,1024]{1,0:T(8,128)(2,1)} async-done(((bf16[256,1024]{1,0:T(8,128)(2,1)}), bf16[1024,1024]{1,0:T(8,128)(2,1)}) %all-gather.3.cloned.1.call-update) | async-done | bytes 2097168 | tf_op jit(solution)/shard_map/all_gather | solution.py:84
  126.6 10.4 all-reduce.12.cloned.1.call-done
  141.0 7.1 gather_fusion
  158.9 10.0 mul.339
  177.0 15.4 gather_fusion.2
  192.5 99.9 %all-to-all-done = bf16[8,1,192,2048]{3,2,1,0:T(8,128)(2,1)} async-done(((bf16[8,1,192,2048]{3,2,1,0:T(8,128)(2,1)}), bf16[8,1,192,2048]{3,2,1,0:T(8,128)(2,1)}, u32[]{:S(2)}, u32[]{:S(2)}) %all-to-all-start) | async-done | bytes 6291488 | tf_op jit(solution)/shard_map/all_to_all | solution.py:139
  297.9 10.3 fusion.6
  308.2 127.7 %all-to-all-done.2 = bf16[8,1,192,2048]{3,2,1,0:T(8,128)(2,1)} async-done(((bf16[8,1,192,2048]{3,2,1,0:T(8,128)(2,1)}), bf16[8,1,192,2048]{3,2,1,0:T(8,128)(2,1)}, u32[]{:S(2)}, u32[]{:S(2)}) %all-to-all-start.2) | async-done | bytes 6291488 | tf_op jit(solution)/shard_map/all_to_all | solution.py:185
  435.9 10.9 fusion.4
  446.9 13.4 multiply_convert_fusion.3
  475.7 11.0 fusion.11
  486.7 10.0 add_convert_fusion
  499.9 113.4 %all-to-all-done.1 = bf16[4,2,1,192,2048]{4,3,1,2,0:T(8,128)(2,1)} async-done(((bf16[4,2,1,192,2048]{4,3,1,2,0:T(8,128)(2,1)}), bf16[4,2,1,192,2048]{4,3,1,2,0:T(8,128)(2,1)}, u32[]{:S(2)}, u32[]{:S(2)}) %all-to-all-start.1) | async-done | bytes 6291488 | tf_op jit(solution)/shard_map/all_to_all | solution.py:151
  627.1 10.3 multiply_convert_fusion.8
  642.4 7.2 multiply_convert_fusion.6
  649.6 9.3 fusion.112
  658.9 8.8 bitcast_convert_fusion.4
  667.8 13.8 gather_fusion.1
  681.5 10.0 reshape.288
  691.5 11.1 multiply_reduce_fusion.1
  702.8 53.4 %all-to-all-done.3 = bf16[2,4,192,2048]{3,2,0,1:T(8,128)(2,1)} async-done(((bf16[2,4,192,2048]{3,2,0,1:T(8,128)(2,1)}), bf16[2,4,192,2048]{3,2,0,1:T(8,128)(2,1)}, u32[]{:S(2)}, u32[]{:S(2)}) %all-to-all-start.3) | async-done | bytes 6291488 | tf_op jit(solution)/shard_map/all_to_all | solution.py:198
  756.2 8.8 bitcast_convert_fusion.3
  765.0 13.6 gather_fusion.3
  778.6 9.8 reshape.290
  788.5 8.6 reduce_sum.163
  797.1 8.5 fusion.44
  807.9 18.9 all-reduce.14.cloned.1.call-done
  852.3 11.0 bitcast_convert_fusion
  863.9 10.7 bitcast_convert_fusion.2
  874.7 10.7 bitcast_convert_fusion.1
  900.8 36.4 %reduce-scatter.16.cloned.1.call-done = bf16[256,1024]{0,1:T(8,128)(2,1)} async-done(((bf16[1024,1024]{0,1:T(8,128)(2,1)}), bf16[256,1024]{0,1:T(8,128)(2,1)}) %reduce-scatter.16.cloned.1.call-update) | async-done | bytes 524304 | tf_op jit(solution)/shard_map/reduce_scatter | solution.py:284
  946.0 7.3 fusion.81
  971.9 11.0 fusion.84
  983.0 10.8 fusion.116
  993.9 10.9 fusion.115
  1010.8 63.3 %reduce-scatter.34.cloned.1.call-done = bf16[2,512,704]{1,2,0:T(8,128)(2,1)} async-done(((bf16[2,2048,704]{1,2,0:T(8,128)(2,1)}), bf16[2,512,704]{1,2,0:T(8,128)(2,1)}) %reduce-scatter.34.cloned.1.call-update) | async-done | bytes 1441808 | tf_op jit(solution)/shard_map/reduce_scatter | solution.py:211
  1077.5 65.5 %reduce-scatter.36.cloned.1.call-done = bf16[2,512,704]{1,2,0:T(8,128)(2,1)} async-done(((bf16[2,2048,704]{1,2,0:T(8,128)(2,1)}), bf16[2,512,704]{1,2,0:T(8,128)(2,1)}) %reduce-scatter.36.cloned.1.call-update) | async-done | bytes 1441808 | tf_op jit(solution)/shard_map/reduce_scatter | solution.py:214
  1146.3 20.8 all-reduce.16.cloned.1.call-done
  1169.0 77.4 %all-reduce.5 = (f32[2048]{0:T(1024)S(1)}, f32[2048]{0:T(1024)S(1)}, f32[2048]{0:T(1024)S(1)}) all-reduce(f32[2048]{0:T(1024)S(1)} %get-tuple-element.21, f32[2048]{0:T(1024)S(1)} %get-tuple-element.19, f32[2048]{0:T(1024)S(1)} %bitcast.216), channel_id=4, replica_groups=mesh['dp'=4,'expert'=4,'tensor'=2] {'dp','expert'}, use_global_device_ids=true, to_apply=%region_27.28.clone | all-reduce | flops 6144 | bytes 49152
  1253.9 174.7 %reduce-scatter.24.cloned.1.call-done = f32[128,1024]{1,0:T(8,128)} async-done(((f32[2048,1024]{1,0:T(8,128)}), f32[128,1024]{1,0:T(8,128)}) %reduce-scatter.24.cloned.1.call-update) | async-done | bytes 524304 | tf_op jit(solution)/shard_map/reduce_scatter | solution.py:312
  1428.6 182.7 %reduce-scatter.18.cloned.1.call-done = f32[128,1024]{1,0:T(8,128)} async-done(((f32[2048,1024]{1,0:T(8,128)}), f32[128,1024]{1,0:T(8,128)}) %reduce-scatter.18.cloned.1.call-update) | async-done | bytes 524304 | tf_op jit(solution)/shard_map/reduce_scatter | solution.py:309
  1611.3 182.6 %reduce-scatter.22.cloned.1.call-done = f32[128,1024]{1,0:T(8,128)} async-done(((f32[2048,1024]{1,0:T(8,128)}), f32[128,1024]{1,0:T(8,128)}) %reduce-scatter.22.cloned.1.call-update) | async-done | bytes 524304 | tf_op jit(solution)/shard_map/reduce_scatter | solution.py:311
  1793.9 182.6 %reduce-scatter.20.cloned.1.call-done = f32[128,1024]{1,0:T(8,128)} async-done(((f32[2048,1024]{1,0:T(8,128)}), f32[128,1024]{1,0:T(8,128)}) %reduce-scatter.20.cloned.1.call-update) | async-done | bytes 524304 | tf_op jit(solution)/shard_map/reduce_scatter | solution.py:310
  1976.5 476.0 %reduce-scatter.32.cloned.1.call-done = f32[128,2816]{1,0:T(8,128)} async-done(((f32[2048,2816]{1,0:T(8,128)}), f32[128,2816]{1,0:T(8,128)}) %reduce-scatter.32.cloned.1.call-update) | async-done | bytes 1441808 | tf_op jit(solution)/shard_map/reduce_scatter | solution.py:318
  2452.4 478.4 %reduce-scatter.30.cloned.1.call-done = f32[128,2816]{1,0:T(8,128)} async-done(((f32[2048,2816]{1,0:T(8,128)}), f32[128,2816]{1,0:T(8,128)}) %reduce-scatter.30.cloned.1.call-update) | async-done | bytes 1441808 | tf_op jit(solution)/shard_map/reduce_scatter | solution.py:317
  2930.9 478.4 %reduce-scatter.28.cloned.1.call-done = f32[128,2816]{1,0:T(8,128)} async-done(((f32[2048,2816]{1,0:T(8,128)}), f32[128,2816]{1,0:T(8,128)}) %reduce-scatter.28.cloned.1.call-update) | async-done | bytes 1441808 | tf_op jit(solution)/shard_map/reduce_scatter | solution.py:316
  (264 shorter events, 203.3 us)
Async XLA Ops:
  7.2 161.8 %copy-start = (bf16[2048,8]{0,1:T(8,128)(2,1)S(1)}, bf16[2048,8]{0,1:T(8,128)(2,1)}, u32[]{:S(2)}) copy-start(bf16[2048,8]{0,1:T(8,128)(2,1)} %param.27) | copy-start | bytes 98308
  7.2 55.9 %all-gather.5.cloned.1.call-start = ((), (), s32[]{:S(2)}) async-start(), calls=%async_computation.18 | async-start | bytes 2621440 | tf_op jit(solution)/shard_map/all_gather | solution.py:83
  8.8 10.2 copy-start.27
  14.2 95.7 %all-gather.3.cloned.1.call-start = ((), (), s32[]{:S(2)}) async-start(), calls=%async_computation.17 | async-start | bytes 2621440 | tf_op jit(solution)/shard_map/all_gather | solution.py:84
  18.6 118.3 %all-reduce.12.cloned.1.call-start = ((), (), s32[]{:S(2)}) async-start(), calls=%async_computation.19 | async-start | bytes 2097152 | tf_op jit(solution)/shard_map/psum | solution.py:114
  69.4 40.5 %copy-start.31 = (f32[8,256]{1,0:T(8,128)}, f32[8,256]{1,0:T(8,128)S(1)}, u32[]{:S(2)}) copy-start(f32[8,256]{1,0:T(8,128)S(1)} %get-tuple-element.46) | copy-start | bytes 24580
  74.6 41.5 %copy-start.37 = (f32[8,256]{1,0:T(8,128)}, f32[8,256]{1,0:T(8,128)S(1)}, u32[]{:S(2)}) copy-start(f32[8,256]{1,0:T(8,128)S(1)} %fusion) | copy-start | bytes 24580
  118.6 22.3 copy-start.23
  140.9 486.2 %copy-start.4 = (bf16[256,2048]{1,0:T(8,128)(2,1)}, bf16[256,2048]{1,0:T(8,128)(2,1)S(1)}, u32[]{:S(2)}) copy-start(bf16[256,2048]{1,0:T(8,128)(2,1)S(1)} %multiply_convert_fusion.10) | copy-start | bytes 3145732
  148.1 144.3 %all-to-all-start = ((bf16[8,1,192,2048]{3,2,1,0:T(8,128)(2,1)}), bf16[8,1,192,2048]{3,2,1,0:T(8,128)(2,1)}, u32[]{:S(2)}, u32[]{:S(2)}) async-start(bf16[8,1,192,2048]{3,2,1,0:T(8,128)(2,1)} %bitcast.200), calls=%async_computation | async-start | bytes 12582912 | tf_op jit(solution)/shard_map/all_to_all | solution.py:139
  292.4 143.5 %all-to-all-start.2 = ((bf16[8,1,192,2048]{3,2,1,0:T(8,128)(2,1)}), bf16[8,1,192,2048]{3,2,1,0:T(8,128)(2,1)}, u32[]{:S(2)}, u32[]{:S(2)}) async-start(bf16[8,1,192,2048]{3,2,1,0:T(8,128)(2,1)} %bitcast.201), calls=%async_computation.2 | async-start | bytes 12582912 | tf_op jit(solution)/shard_map/all_to_all | solution.py:185
  435.9 24.4 slice-start.5
  446.9 13.4 slice-start.6
  470.0 143.3 %all-to-all-start.1 = ((bf16[4,2,1,192,2048]{4,3,1,2,0:T(8,128)(2,1)}), bf16[4,2,1,192,2048]{4,3,1,2,0:T(8,128)(2,1)}, u32[]{:S(2)}, u32[]{:S(2)}) async-start(bf16[4,2,1,192,2048]{4,3,1,2,0:T(8,128)(2,1)} %pad_maximum_fusion), calls=%async_computation.1 | async-start | bytes 12582912 | tf_op jit(solution)/shard_map/all_to_all | solution.py:151
  475.7 11.0 copy-start.51
  499.9 118.7 %copy-start.41 = (bf16[2048]{0:T(1024)(128)(2,1)S(1)}, bf16[2048]{0:T(1024)(128)(2,1)}, u32[]{:S(2)}) copy-start(bf16[2048]{0:T(1024)(128)(2,1)} %param.28) | copy-start | bytes 12292
  613.3 142.9 %all-to-all-start.3 = ((bf16[2,4,192,2048]{3,2,0,1:T(8,128)(2,1)}), bf16[2,4,192,2048]{3,2,0,1:T(8,128)(2,1)}, u32[]{:S(2)}, u32[]{:S(2)}) async-start(bf16[2,4,192,2048]{3,2,0,1:T(8,128)(2,1)} %copy.136), calls=%async_computation.3 | async-start | bytes 12582912 | tf_op jit(solution)/shard_map/all_to_all | solution.py:198
  618.6 208.3 %all-reduce.14.cloned.1.call-start = ((), (), s32[]{:S(2)}) async-start(), calls=%async_computation.20 | async-start | bytes 2097152 | tf_op jit(solution)/shard_map/psum | solution.py:236
  620.6 16.8 slice-start.2
  620.6 16.8 slice-start.3
  627.0 10.3 copy-start.50
  627.0 10.3 slice-start.4
  681.5 10.0 copy-start.21
  691.5 11.2 copy-start.34
  691.5 11.3 copy-start.26
  691.5 11.3 copy-start.40
  691.5 11.2 copy-start.43
  805.6 21.2 copy-start.3
  805.6 21.2 copy-start.9
  805.6 21.2 copy-start.24
  805.6 21.2 copy-start.36
  807.8 87.3 %reduce-scatter.14.cloned.1.call-start = ((), (), s32[]{:S(2)}) async-start(), calls=%async_computation.21 | async-start | bytes 2621440 | tf_op jit(solution)/shard_map/reduce_scatter | solution.py:278
  845.9 91.3 %reduce-scatter.16.cloned.1.call-start = ((), (), s32[]{:S(2)}) async-start(), calls=%async_computation.22 | async-start | bytes 2621440 | tf_op jit(solution)/shard_map/reduce_scatter | solution.py:284
  852.3 155.2 %reduce-scatter.38.cloned.1.call-start = ((), (), s32[]{:S(2)}) async-start(), calls=%async_computation.33 | async-start | bytes 7208960 | tf_op jit(solution)/shard_map/reduce_scatter | solution.py:217
  863.4 210.8 %reduce-scatter.34.cloned.1.call-start = ((), (), s32[]{:S(2)}) async-start(), calls=%async_computation.31 | async-start | bytes 7208960 | tf_op jit(solution)/shard_map/reduce_scatter | solution.py:211
  874.6 268.4 %reduce-scatter.36.cloned.1.call-start = ((), (), s32[]{:S(2)}) async-start(), calls=%async_computation.32 | async-start | bytes 7208960 | tf_op jit(solution)/shard_map/reduce_scatter | solution.py:214
  885.4 281.7 %all-reduce.16.cloned.1.call-start = ((), (), s32[]{:S(2)}) async-start(), calls=%async_computation.34 | async-start | bytes 4194304 | tf_op jit(solution)/shard_map/psum | solution.py:159
  900.8 41.8 %copy-start.45 = (bf16[256]{0:T(256)(128)(2,1)S(1)}, bf16[256]{0:T(256)(128)(2,1)}, u32[]{:S(2)}) copy-start(bf16[256]{0:T(256)(128)(2,1)} %get-tuple-element.30) | copy-start | bytes 1540
  900.8 44.3 %copy-start.5 = (bf16[256,2048]{1,0:T(8,128)(2,1)S(1)}, bf16[256,2048]{1,0:T(8,128)(2,1)}, u32[]{:S(2)}) copy-start(bf16[256,2048]{1,0:T(8,128)(2,1)} %copy-done.4) | copy-start | bytes 3145732
  942.5 311.4 %reduce-scatter.26.cloned.1.call-start = ((), (), s32[]{:S(2)}) async-start(), calls=%async_computation.27 | async-start | bytes 69632 | tf_op jit(solution)/shard_map/reduce_scatter | solution.py:314
  946.0 482.6 %reduce-scatter.24.cloned.1.call-start = ((), (), s32[]{:S(2)}) async-start(), calls=%async_computation.26 | async-start | bytes 8912896 | tf_op jit(solution)/shard_map/reduce_scatter | solution.py:312
  953.4 657.9 %reduce-scatter.18.cloned.1.call-start = ((), (), s32[]{:S(2)}) async-start(), calls=%async_computation.23 | async-start | bytes 8912896 | tf_op jit(solution)/shard_map/reduce_scatter | solution.py:309
  960.0 833.9 %reduce-scatter.22.cloned.1.call-start = ((), (), s32[]{:S(2)}) async-start(), calls=%async_computation.25 | async-start | bytes 8912896 | tf_op jit(solution)/shard_map/reduce_scatter | solution.py:311
  965.8 1010.6 %reduce-scatter.20.cloned.1.call-start = ((), (), s32[]{:S(2)}) async-start(), calls=%async_computation.24 | async-start | bytes 8912896 | tf_op jit(solution)/shard_map/reduce_scatter | solution.py:310
  971.7 1480.8 %reduce-scatter.32.cloned.1.call-start = ((), (), s32[]{:S(2)}) async-start(), calls=%async_computation.30 | async-start | bytes 24510464 | tf_op jit(solution)/shard_map/reduce_scatter | solution.py:318
  983.0 1947.9 %reduce-scatter.30.cloned.1.call-start = ((), (), s32[]{:S(2)}) async-start(), calls=%async_computation.29 | async-start | bytes 24510464 | tf_op jit(solution)/shard_map/reduce_scatter | solution.py:317
  993.8 2415.5 %reduce-scatter.28.cloned.1.call-start = ((), (), s32[]{:S(2)}) async-start(), calls=%async_computation.28 | async-start | bytes 24510464 | tf_op jit(solution)/shard_map/reduce_scatter | solution.py:316
  1077.5 170.6 %copy-start.10 = (bf16[256,2048]{1,0:T(8,128)(2,1)S(1)}, bf16[256,2048]{1,0:T(8,128)(2,1)}, u32[]{:S(2)}) copy-start(bf16[256,2048]{1,0:T(8,128)(2,1)} %all-reduce.12.cloned.1.call-done) | copy-start | bytes 3145732
  (34 other events, 131.6 us)
Sparse Core Ops, SparseCore 0:
  14.3 48.7 all-gather.4
  65.2 44.6 all-gather.2
  118.6 18.3 all-reduce.11
  807.9 18.8 all-reduce.13
  846.0 45.0 reduce-scatter.13
  893.9 43.1 reduce-scatter.15
  940.2 65.1 reduce-scatter.37
  1008.3 65.8 reduce-scatter.33
  1077.2 65.8 reduce-scatter.35
  1145.8 21.2 all-reduce.15
  1170.0 76.9 reduce-scatter.25
  1249.8 178.8 reduce-scatter.23
  1431.5 179.8 reduce-scatter.17
  1614.1 179.8 reduce-scatter.21
  1796.6 179.8 reduce-scatter.19
  1979.2 473.1 reduce-scatter.31
  2455.2 475.6 reduce-scatter.29
  2933.6 475.6 reduce-scatter.27
